TPU v7x, 32 devices: a whole 2x2x4 slice. The times are simulated.
32 devices in a mesh: group: 4 (over y, x), dev: 8 (over z, core).
Axes of the slice: x: 2, y: 2, z: 4, core: 2. Of those that a mesh axis runs over, the one named last changes fastest.
Arguments:
- density: float32 [32, 320, 128], P(('group', 'dev')), may hold values from 0.5 to 2
- velocity: float32 [3, 32, 320, 128], P(None, ('group', 'dev')), may hold values from -0.75 to 0.75
- pressure: float32 [32, 320, 128], P(('group', 'dev')), may hold values from 0.5 to 2
- rbf_blocks: bfloat16 [2048, 128, 128], P(('group', 'dev')), may hold values from -0.5 to 0.5
- correlation: int32 [2048, 128], P(('group', 'dev')), may hold values from 0 to 319
- normals: float32 [2048, 3, 128], P(('group', 'dev')), may hold values from -6 to 6
- routes: int32 [2048, 1], P(('group', 'dev')), may hold values from 0 to 31; in each aligned block of 64 rows (0 to 63, 64 to 127, ...) at most 4 rows name the same one
- targets: int32 [2048], P(('group', 'dev')), may hold values from 0 to 31
- stiffness: bfloat16 [1024, 128, 128], P(('group', 'dev')), may hold values from -0.35 to 2.35
- coupling: bfloat16 [1024, 128, 128], P(('group', 'dev')), may hold values from -0.5 to 0.5
- inverse_diag: float32 [1024, 3, 128], P(('group', 'dev')), may hold values from 0.5 to 1.5
- displacement: float32 [1024, 3, 128], P(('group', 'dev')), may hold values from -6 to 6
- diff_res: float32 [8, 1024, 3, 128], P(None, ('group', 'dev')), may hold values from -2 to 2
- diff_disp: float32 [8, 1024, 3, 128], P(None, ('group', 'dev')), may hold values from -2.4 to 2.4
Outputs:
- fluid_next: float32 [5, 32, 320, 128], P(None, ('group', 'dev'))
- disp_next: float32 [1024, 3, 128], P(('group', 'dev'))
- wall_motion: float32 [2048, 3, 128], P(('group', 'dev'))
Inputs may be any that keep to these rules, and one draw needn't show every extreme that they name: `routes`: among the 64 blocks of one device at most 4 name the same owner, and some device names one owner exactly 4 times.
All inputs are finite; a program needn't handle non-finite values.
Results may differ from a plain program's by a relative error of at most 0.0004.
The roundings to bfloat16 on the way count: a program that leaves them out, or rounds other values in their place, can miss the bound.
Values may be sent and summed in bfloat16 or wider, within the bound.
A program may use at most 64 MiB of HBM per device.

v0:
```python
import functools

import jax
import jax.numpy as jnp
from jax import lax
from jax.experimental import pallas as pl
from jax.experimental.pallas import tpu as pltpu
from jax.sharding import PartitionSpec as P

ratio_heat = 1.4
step_ratio = 0.03
AXES = ("group", "dev")
MESH = pl.DeviceIdType.MESH
LAST = (((1,), (1,)), ((), ()))


def conserve(prim):
    dens, u, v, w, press = prim
    energy = press / (ratio_heat - 1.0) + 0.5 * dens * (u * u + v * v + w * w)
    return (dens, dens * u, dens * v, dens * w, energy)


def flux_parts(prim, axis):
    state = conserve(prim)
    normal = prim[1 + axis]
    press = prim[4]
    rows = [row * normal for row in state]
    rows[1 + axis] = rows[1 + axis] + press
    rows[4] = rows[4] + press * normal
    speed = jnp.abs(normal) + jnp.sqrt(ratio_heat * press / prim[0])
    return state, rows, speed


def face_difference(low, mid, high, axis):
    state_l, flux_l, speed_l = flux_parts(low, axis)
    state_m, _, speed_m = flux_parts(mid, axis)
    state_h, flux_h, speed_h = flux_parts(high, axis)
    upper = jnp.maximum(speed_m, speed_h)
    lower = jnp.maximum(speed_l, speed_m)
    return [
        0.5 * (fh - fl) - 0.5 * (upper * (sh - sm) - lower * (sm - sl))
        for fh, fl, sh, sm, sl in zip(flux_h, flux_l, state_h, state_m, state_l)
    ]


def advance(mid, x_pair, y_pair, z_pair):
    div_x = face_difference(x_pair[0], mid, x_pair[1], 0)
    div_y = face_difference(y_pair[0], mid, y_pair[1], 1)
    div_z = face_difference(z_pair[0], mid, z_pair[1], 2)
    return [
        row - step_ratio * (a + b + c)
        for row, a, b, c in zip(conserve(mid), div_x, div_y, div_z)
    ]


def flow_kernel(dens_ref, vel_ref, press_ref, low_ref, high_ref, out_ref):
    height, lanes = dens_ref.shape[1:]
    chunk = next(c for c in (32, 16, 8, height) if height % c == 0)
    row = lax.broadcasted_iota(jnp.int32, (chunk, lanes), 0)
    lane = lax.broadcasted_iota(jnp.int32, (chunk, lanes), 1)
    fields = [dens_ref.at[0]] + [vel_ref.at[i, 0] for i in range(3)] + [press_ref.at[0]]
    for start in range(0, height, chunk):
        rows = slice(start, start + chunk)
        before = (start - 1) % height
        after = (start + chunk) % height
        mid = [f[rows, :] for f in fields]
        y_low = [
            jnp.where(row == 0, f[before : before + 1, :], pltpu.roll(m, 1, 0))
            for f, m in zip(fields, mid)
        ]
        y_high = [
            jnp.where(row == chunk - 1, f[after : after + 1, :], pltpu.roll(m, chunk - 1, 0))
            for f, m in zip(fields, mid)
        ]
        signs = (1.0, 1.0, 1.0, -1.0, 1.0)
        z_low = [jnp.where(lane == 0, s * m, pltpu.roll(m, 1, 1)) for s, m in zip(signs, mid)]
        z_high = [jnp.where(lane == lanes - 1, m, pltpu.roll(m, lanes - 1, 1)) for m in mid]
        x_low = [low_ref[i, rows, :].astype(jnp.float32) for i in range(5)]
        x_high = [high_ref[i, rows, :].astype(jnp.float32) for i in range(5)]
        result = advance(mid, (x_low, x_high), (y_low, y_high), (z_low, z_high))
        for i in range(5):
            out_ref[i, 0, rows, :] = result[i]


def prepare_kernel(
    capacity,
    dens_ref,
    vel_ref,
    press_ref,
    owner_row_ref,
    target_ref,
    ends_ref,
    prim_ref,
    pick_ref,
    place_ref,
    tags_ref,
    column,
):
    height, lanes = dens_ref.shape[1:]
    fields = [dens_ref.at[0]] + [vel_ref.at[i, 0] for i in range(3)] + [press_ref.at[0]]
    ends_ref[...] = jnp.ones_like(ends_ref)
    column[...] = jnp.ones_like(column)
    for i, field in enumerate(fields):
        value = field[...]
        prim_ref[i] = value.astype(jnp.bfloat16)
        column[0:height, :] = value
        for start in range(0, column.shape[0], lanes):
            turned = column[start : start + lanes, :].T
            for z in range(2):
                ends_ref[z, i : i + 1, start : start + lanes] = turned[z : z + 1, :]
    edge = ends_ref[0]
    total = edge.shape[1]
    lane = lax.broadcasted_iota(jnp.int32, edge.shape, 1)
    ends_ref[2] = jnp.where(lane == height - 1, edge[:, 0:1], pltpu.roll(edge, total - 1, 1))
    ends_ref[3] = jnp.where(lane == 0, edge[:, height - 1 : height], pltpu.roll(edge, 1, 1))

    blocks, slot_count = pick_ref.shape
    owner_row = owner_row_ref[...].astype(jnp.float32)
    row_id = lax.broadcasted_iota(jnp.int32, (blocks, blocks), 0)
    column_id = lax.broadcasted_iota(jnp.int32, (blocks, blocks), 1)
    owner = jnp.sum(jnp.where(row_id == column_id, owner_row, 0.0), axis=1, keepdims=True)
    same = jnp.where(owner == owner_row, 1.0, 0.0)
    rank = jnp.sum(jnp.where(column_id < row_id, same, 0.0), axis=1, keepdims=True)
    rank_row = jnp.sum(jnp.where(row_id < column_id, same, 0.0), axis=0, keepdims=True)
    slot = owner * capacity + rank
    slot_row = owner_row * capacity + rank_row
    lane_id = lax.broadcasted_iota(jnp.int32, (blocks, slot_count), 1).astype(jnp.float32)
    pick_ref[...] = jnp.where(slot == lane_id, 1.0, 0.0).astype(jnp.bfloat16)
    line_id = lax.broadcasted_iota(jnp.int32, (slot_count, blocks), 0).astype(jnp.float32)
    placed = jnp.where(slot_row == line_id, 1.0, 0.0)
    place_ref[...] = placed.astype(jnp.bfloat16)
    tag = jnp.sum(placed * (target_ref[...].astype(jnp.float32) + 1.0), axis=1, keepdims=True)
    tag = jnp.broadcast_to(tag - 1.0, (slot_count, tags_ref.shape[2]))
    for p in range(tags_ref.shape[0]):
        tags_ref[p] = tag[p * capacity : (p + 1) * capacity, :]


def thirds(value):
    high = value.astype(jnp.bfloat16)
    rest = value - high.astype(jnp.float32)
    middle = rest.astype(jnp.bfloat16)
    low = (rest - middle.astype(jnp.float32)).astype(jnp.bfloat16)
    return high, middle, low


def select_rows(chooser, value):
    parts = [
        jnp.dot(chooser, part, preferred_element_type=jnp.float32) for part in thirds(value)
    ]
    return (parts[2] + parts[1]) + parts[0]


def couple_kernel(
    peers,
    width,
    wall_ref,
    prim_ref,
    normals_ref,
    index_ref,
    rbf_ref,
    pick_ref,
    place_ref,
    tags_ref,
    stiff_ref,
    coup_ref,
    inv_ref,
    disp_ref,
    res_ref,
    dif_ref,
    dens_ref,
    vel_ref,
    press_ref,
    fluid_ref,
    next_ref,
    motion_ref,
    low_ref,
    high_ref,
    side_ref,
    prior_ref,
    tag_in,
    load_out,
    load_in,
    reply_out,
    reply_in,
    stat_out,
    stat_in,
    loads,
    slots,
    solid,
    products,
    near_send,
    near_recv,
    tag_send,
    tag_recv,
    load_send,
    load_recv,
    stat_send,
    stat_recv,
    reply_send,
    reply_recv,
):
    me = lax.axis_index("group") * width + lax.axis_index("dev")
    blocks = index_ref.shape[0]
    count = disp_ref.shape[1]
    columns = res_ref.shape[0]
    capacity = tags_ref.shape[1]
    nodes = index_ref.shape[1]

    def place(peer):
        return (peer // width, peer % width)

    def hop(distance):
        return (me + distance) % peers

    barrier = pltpu.get_barrier_semaphore()

    def greet(step, carry):
        pl.semaphore_signal(barrier, inc=1, device_id=place(hop(step)), device_id_type=MESH)
        return carry

    lax.fori_loop(1, peers, greet, 0)
    products[...] = jnp.zeros_like(products)
    for m in range(columns):
        for n in range(m, columns):
            line = jnp.sum(jnp.sum(res_ref[m] * res_ref[n], axis=0), axis=0, keepdims=True)
            products[m * columns + n : m * columns + n + 1, :] = line
            products[n * columns + m : n * columns + m + 1, :] = line
    pl.semaphore_wait(barrier, peers - 1)

    def near(slot, src, dst, distance):
        return pltpu.make_async_remote_copy(
            src_ref=src,
            dst_ref=dst,
            send_sem=near_send.at[slot],
            recv_sem=near_recv.at[slot],
            device_id=place(hop(distance)),
            device_id_type=MESH,
        )

    wall_up = near(0, wall_ref.at[0], side_ref.at[0], 1)
    wall_down = near(1, wall_ref.at[0], side_ref.at[1], peers - 1)
    tail = prior_ref.shape[1]
    prior = near(2, disp_ref.at[:, pl.ds(count - tail, tail), :], prior_ref, 1)
    early, late = pl.ds(0, 3), pl.ds(3, 2)
    bulk_early = (
        near(3, prim_ref.at[early], low_ref.at[early], 1),
        near(4, prim_ref.at[early], high_ref.at[early], peers - 1),
    )
    bulk_late = (
        near(5, prim_ref.at[late], low_ref.at[late], 1),
        near(6, prim_ref.at[late], high_ref.at[late], peers - 1),
    )

    def spread(src, dst, send, recv, indexed):
        def begin(step, carry):
            peer = hop(step)
            pltpu.make_async_remote_copy(
                src_ref=src.at[peer] if indexed else src,
                dst_ref=dst.at[me],
                send_sem=send.at[step],
                recv_sem=recv.at[step],
                device_id=place(peer),
                device_id_type=MESH,
            ).start()
            return carry

        lax.fori_loop(1, peers, begin, 0)

    def gather(src, dst, send, recv, indexed):
        def finish(step, carry):
            pltpu.make_async_remote_copy(
                src_ref=src.at[hop(step)] if indexed else src,
                dst_ref=dst.at[hop(peers - step)],
                send_sem=send.at[step],
                recv_sem=recv.at[step],
                device_id=place(hop(step)),
                device_id_type=MESH,
            ).wait()
            return carry

        lax.fori_loop(1, peers, finish, 0)

    wall_up.start()
    wall_down.start()
    prior.start()
    spread(tags_ref, tag_in, tag_send, tag_recv, True)
    for copy in bulk_early:
        copy.start()
    tag_in[me] = tags_ref[me]

    wall_up.wait()
    wall_down.wait()

    def variant(i):
        return [wall_ref[i, k : k + 1, :] for k in range(5)]

    mid = variant(0)
    mirror = list(mid)
    mirror[3] = -mirror[3]
    beside = [[side_ref[j, k : k + 1, :] for k in range(5)] for j in range(2)]
    bottom = advance(mid, beside, (variant(3), variant(2)), (mirror, variant(1)))
    kinetic = bottom[1] * bottom[1] + bottom[2] * bottom[2] + bottom[3] * bottom[3]
    wall = (ratio_heat - 1.0) * (bottom[4] - 0.5 * kinetic / bottom[0])

    index = index_ref[...]
    low = index % nodes
    found = jnp.zeros(index.shape, jnp.float32)
    for part in range(wall.shape[1] // nodes):
        source = jnp.broadcast_to(wall[:, part * nodes : (part + 1) * nodes], index.shape)
        taken = jnp.take_along_axis(source, low, axis=1)
        found = jnp.where(index // nodes == part, taken, found)
    for c in range(3):
        loads[:, c, :] = found * normals_ref[c]
    for b in range(blocks):
        weighted = loads[b, 0:3, :].astype(jnp.bfloat16)
        loads[b, 0:3, :] = jnp.dot(weighted, rbf_ref[b], preferred_element_type=jnp.float32)
    spans = [slice(c * nodes, (c + 1) * nodes) for c in range(3)]
    for c in range(3):
        slots[:, spans[c]] = select_rows(place_ref[...], loads[:, c, :])
    for p in range(peers):
        load_out[p] = slots[p * capacity : (p + 1) * capacity, :]
    spread(load_out, load_in, load_send, load_recv, True)
    load_in[me] = load_out[me]

    prior.wait()
    first = (me > 0).astype(jnp.float32)
    for c in range(3):
        solid[:, c, :] = disp_ref[c]
    for t in range(count - 1, -1, -1):
        half = solid[t, 0:3, :].astype(jnp.bfloat16)
        earlier = solid[t - 1, 0:3, :] if t else prior_ref[:, tail - 1, :] * first
        part = lax.dot_general(half, stiff_ref[t], LAST, preferred_element_type=jnp.float32)
        part = part + lax.dot_general(
            earlier.astype(jnp.bfloat16), coup_ref[t], LAST, preferred_element_type=jnp.float32
        )
        solid[t, 0:3, :] = part

    gather(tags_ref, tag_in, tag_send, tag_recv, True)
    for p in range(peers):
        slots[p * capacity : (p + 1) * capacity, spans[0]] = tag_in[p]
    tags = slots[:, spans[0]]
    lane = lax.broadcasted_iota(jnp.int32, tags.shape, 1).astype(jnp.float32)
    chooser = (tags == lane).astype(jnp.float32)[:, 0:count].astype(jnp.bfloat16)
    turned = tags.T[0:count, :]
    line_id = lax.broadcasted_iota(jnp.int32, turned.shape, 0).astype(jnp.float32)
    collector = (turned == line_id).astype(jnp.float32).astype(jnp.bfloat16)

    gather(load_out, load_in, load_send, load_recv, True)
    for p in range(peers):
        slots[p * capacity : (p + 1) * capacity, :] = load_in[p]
    change = [
        -inv_ref[c] * (solid[:, c, :] - select_rows(collector, slots[:, spans[c]]))
        for c in range(3)
    ]
    for m in range(columns):
        line = sum(res_ref[m, c] * change[c] for c in range(3))
        at = columns * columns + m
        products[at : at + 1, :] = jnp.sum(line, axis=0, keepdims=True)
    stat_out[...] = jnp.sum(products[...].T, axis=0, keepdims=True)
    spread(stat_out, stat_in, stat_send, stat_recv, False)
    for copy in bulk_late:
        copy.start()
    stat_in[me] = stat_out[...]
    for c in range(3):
        next_ref[c] = disp_ref[c] + change[c]
    gather(stat_out, stat_in, stat_send, stat_recv, False)
    total = jnp.sum(stat_in[...], axis=0)
    shape = (columns, nodes)
    m_id = lax.broadcasted_iota(jnp.int32, shape, 0)
    n_id = lax.broadcasted_iota(jnp.int32, shape, 1)
    source = jnp.where(
        n_id < columns, m_id * columns + n_id, columns * columns + m_id
    )
    matrix = jnp.take_along_axis(jnp.broadcast_to(total, shape), source, axis=1)
    for k in range(columns):
        line = matrix[k : k + 1, :]
        scaled = line / matrix[k : k + 1, k : k + 1]
        matrix = jnp.where(m_id == k, scaled, matrix - matrix[:, k : k + 1] * scaled)
    mixing = -matrix[:, columns : columns + 1]
    for c in range(3):
        result = next_ref[c]
        for m in range(columns):
            result = result + dif_ref[m, c] * mixing[m : m + 1, :]
        next_ref[c] = result
        slots[:, spans[c]] = jnp.dot(
            chooser, result.astype(jnp.bfloat16), preferred_element_type=jnp.float32
        )
    for p in range(peers):
        reply_out[p] = slots[p * capacity : (p + 1) * capacity, :].astype(jnp.bfloat16)
    spread(reply_out, reply_in, reply_send, reply_recv, True)
    reply_in[me] = reply_out[me]
    for copy in bulk_early + bulk_late:
        copy.wait()
    flow_kernel(dens_ref, vel_ref, press_ref, low_ref, high_ref, fluid_ref)
    gather(reply_out, reply_in, reply_send, reply_recv, True)
    for p in range(peers):
        slots[p * capacity : (p + 1) * capacity, :] = reply_in[p].astype(jnp.float32)
    for c in range(3):
        rows = slots[:, spans[c]].astype(jnp.bfloat16)
        loads[:, c, :] = jnp.dot(pick_ref[...], rows, preferred_element_type=jnp.float32)
    for b in range(blocks):
        reply = loads[b, 0:3, :].astype(jnp.bfloat16)
        loads[b, 0:3, :] = lax.dot_general(
            reply, rbf_ref[b], LAST, preferred_element_type=jnp.float32
        )
    for c in range(3):
        motion_ref[c] = loads[:, c, :]


def rows_last(value):
    return jnp.swapaxes(value, -3, -2)


def on_device(
    density,
    velocity,
    pressure,
    rbf_blocks,
    correlation,
    normals,
    routes,
    targets,
    stiffness,
    coupling,
    inverse_diag,
    displacement,
    diff_res,
    diff_disp,
):
    f32, bf16 = jnp.float32, jnp.bfloat16
    width = lax.axis_size("dev")
    peers = lax.axis_size(AXES)
    blocks, nodes = correlation.shape
    count = displacement.shape[0]
    columns = diff_res.shape[0]
    height, depth = density.shape[1:]
    capacity = max(2, 2 * blocks // peers)
    slot_count = peers * capacity

    padded = -(-height // depth) * depth
    halo = jax.ShapeDtypeStruct((5, height, depth), bf16)
    vmem = pl.BlockSpec(memory_space=pltpu.VMEM)
    anywhere = pl.BlockSpec(memory_space=pl.ANY)
    dma = pltpu.SemaphoreType.DMA
    ends, prim, pick, put, tags = pl.pallas_call(
        functools.partial(prepare_kernel, capacity),
        out_shape=(
            jax.ShapeDtypeStruct((4, 8, padded), f32),
            halo,
            jax.ShapeDtypeStruct((blocks, slot_count), bf16),
            jax.ShapeDtypeStruct((slot_count, blocks), bf16),
            jax.ShapeDtypeStruct((peers, capacity, nodes), f32),
        ),
        in_specs=[vmem] * 5,
        out_specs=(vmem,) * 5,
        scratch_shapes=[pltpu.VMEM((padded, depth), f32)],
    )(density, velocity, pressure, routes.reshape(1, blocks), targets.reshape(1, blocks))
    width_row = 3 * nodes
    fluid_next, disp_next, wall_motion = pl.pallas_call(
        functools.partial(couple_kernel, peers, width),
        out_shape=(
            jax.ShapeDtypeStruct((5,) + density.shape, f32),
            jax.ShapeDtypeStruct((3, count, nodes), f32),
            jax.ShapeDtypeStruct((3, blocks, nodes), f32),
        ),
        in_specs=[vmem, anywhere] + [vmem] * 15,
        out_specs=(vmem, vmem, vmem),
        scratch_shapes=[
            pltpu.VMEM(halo.shape, bf16),
            pltpu.VMEM(halo.shape, bf16),
            pltpu.VMEM((2, 8, padded), f32),
            pltpu.VMEM((3, 8, nodes), f32),
            pltpu.VMEM((peers, capacity, nodes), f32),
            pltpu.VMEM((peers, capacity, width_row), f32),
            pltpu.VMEM((peers, capacity, width_row), f32),
            pltpu.VMEM((peers, capacity, width_row), bf16),
            pltpu.VMEM((peers, capacity, width_row), bf16),
            pltpu.VMEM((1, nodes), f32),
            pltpu.VMEM((peers, 1, nodes), f32),
            pltpu.VMEM((blocks, 8, nodes), f32),
            pltpu.VMEM((slot_count, width_row), f32),
            pltpu.VMEM((count, 8, nodes), f32),
            pltpu.VMEM((nodes, nodes), f32),
            dma((7,)),
            dma((7,)),
        ]
        + [dma((peers,))] * 8,
        compiler_params=pltpu.CompilerParams(collective_id=0, has_side_effects=True),
    )(
        ends,
        prim,
        rows_last(normals),
        correlation,
        rbf_blocks,
        pick,
        put,
        tags,
        stiffness,
        coupling,
        rows_last(inverse_diag),
        rows_last(displacement),
        rows_last(diff_res),
        rows_last(diff_disp),
        density,
        velocity,
        pressure,
    )
    return (fluid_next, rows_last(disp_next), rows_last(wall_motion))


def solution(mesh):
    placed = (
        P(("group", "dev"), None, None),
        P(None, ("group", "dev"), None, None),
        P(("group", "dev"), None, None),
        P(("group", "dev"), None, None),
        P(("group", "dev"), None),
        P(("group", "dev"), None, None),
        P(("group", "dev"), None),
        P(("group", "dev")),
        P(("group", "dev"), None, None),
        P(("group", "dev"), None, None),
        P(("group", "dev"), None, None),
        P(("group", "dev"), None, None),
        P(None, ("group", "dev"), None, None),
        P(None, ("group", "dev"), None, None),
    )
    return jax.shard_map(
        on_device,
        mesh=mesh,
        in_specs=placed,
        out_specs=(
            P(None, ("group", "dev"), None, None),
            P(("group", "dev"), None, None),
            P(("group", "dev"), None, None),
        ),
        check_vma=False,
    )
```

profile of v0, /device:TPU:0, one launch (start us, length us, event | category | flops | bytes accessed | tf_op | source)
XLA Modules:
  0.0 46.9 jit_solution(16536158168566342315)
XLA Ops:
  0.6 2.2 %shard_map.157 = (f32[4,8,384]{2,1,0:T(8,128)}, bf16[5,320,128]{2,1,0:T(8,128)(2,1)}, bf16[64,128]{1,0:T(8,128)(2,1)}, bf16[128,64]{1,0:T(8,128)(2,1)}, f32[32,4,128]{2,1,0:T(4,128)}) custom-call(f32[1,320,128]{2,1,0:T(8,128)} %dens_ref.3, f32[3,1,320,128]{3,2,1,0:T(8,128)} %vel_ref.3, f32[1,320,128]{2,1,0:T(8,128)} %press_ref.3, s32[1,64]{1,0:T(1,128)} %bitcast.16, ...), custom_call_target="tpu_custom_call" | custom-call | tf_op jit(solution)/shard_map/pallas_call | solution.py:445
  2.9 38.9 %shard_map.158 = (f32[5,1,320,128]{3,2,1,0:T(8,128)}, f32[3,32,128]{2,1,0:T(8,128)}, f32[3,64,128]{2,1,0:T(8,128)}) custom-call(f32[4,8,384]{2,1,0:T(8,128)} %get-tuple-element.11.wall_ref, bf16[5,320,128]{2,1,0:T(8,128)(2,1)} %get-tuple-element.12.prim_ref, f32[3,64,128]{2,1,0:T(8,128)} %bitcast.12, s32[64,128]{1,0:T(8,128)} %index_ref.1, ...), custom_call_target="tpu_custom_call" | custom-call | tf_op jit(solution)/shard_map/pallas_call | solution.py:459
  41.8 2.1 %copy.20 = f32[5,1,320,128]{3,2,1,0:T(8,128)} copy(f32[5,1,320,128]{3,2,1,0:T(8,128)} %get-tuple-element.22) | data formatting | bytes 1638400
  43.9 1.4 %copy.21 = f32[32,3,128]{2,0,1:T(8,128)} copy(f32[32,3,128]{2,0,1:T(8,128)} %bitcast.15) | data formatting | bytes 98304
  45.3 1.5 %copy.22 = f32[64,3,128]{2,0,1:T(8,128)} copy(f32[64,3,128]{2,0,1:T(8,128)} %bitcast.11) | data formatting | bytes 196608
where the time goes:
time: 47.1 us; the launch traced here: 46.9 us
  Pallas kernels  41.2 us (87%)
  local copies, waits for them, and re-layouts  5.05 us (11%)
  between operations  0.64 us (1%)
    pallas_call x1, Pallas kernels, on_device(): pl.pallas_call(functools.partial(couple_kernel, peers, width), out_shape=...  38.9 us
    unnamed x3, local copies, waits for them, and re-layouts  5.05 us
    pallas_call x1, Pallas kernels, on_device(): pl.pallas_call(functools.partial(prepare_kernel, capacity), out_shape=(ja...  2.24 us

commit v1 on v0

v1 whole, which is shorter than its diff:
```python
import functools

import jax
import jax.numpy as jnp
from jax import lax
from jax.experimental import pallas as pl
from jax.experimental.pallas import tpu as pltpu
from jax.sharding import PartitionSpec as P

ratio_heat = 1.4
step_ratio = 0.03
AXES = ("group", "dev")
LOGICAL = pl.DeviceIdType.LOGICAL
LAST = (((1,), (1,)), ((), ()))
WIDE = 12


def conserve(prim):
    dens, u, v, w, press = prim
    energy = press / (ratio_heat - 1.0) + 0.5 * dens * (u * u + v * v + w * w)
    return (dens, dens * u, dens * v, dens * w, energy)


def flux_parts(prim, axis):
    state = conserve(prim)
    normal = prim[1 + axis]
    press = prim[4]
    rows = [row * normal for row in state]
    rows[1 + axis] = rows[1 + axis] + press
    rows[4] = rows[4] + press * normal
    speed = jnp.abs(normal) + jnp.sqrt(ratio_heat * press / prim[0])
    return state, rows, speed


def face_difference(low, mid, high, axis):
    state_l, flux_l, speed_l = flux_parts(low, axis)
    state_m, _, speed_m = flux_parts(mid, axis)
    state_h, flux_h, speed_h = flux_parts(high, axis)
    upper = jnp.maximum(speed_m, speed_h)
    lower = jnp.maximum(speed_l, speed_m)
    return [
        0.5 * (fh - fl) - 0.5 * (upper * (sh - sm) - lower * (sm - sl))
        for fh, fl, sh, sm, sl in zip(flux_h, flux_l, state_h, state_m, state_l)
    ]


def advance(mid, x_pair, y_pair, z_pair):
    div_x = face_difference(x_pair[0], mid, x_pair[1], 0)
    div_y = face_difference(y_pair[0], mid, y_pair[1], 1)
    div_z = face_difference(z_pair[0], mid, z_pair[1], 2)
    return [
        row - step_ratio * (a + b + c)
        for row, a, b, c in zip(conserve(mid), div_x, div_y, div_z)
    ]


def flow_section(fields, low_ref, high_ref, out_ref):
    height, lanes = fields[0].shape
    chunk = next(c for c in (32, 16, 8, height) if height % c == 0)
    row = lax.broadcasted_iota(jnp.int32, (chunk, lanes), 0)
    lane = lax.broadcasted_iota(jnp.int32, (chunk, lanes), 1)
    for start in range(0, height, chunk):
        rows = slice(start, start + chunk)
        before = (start - 1) % height
        after = (start + chunk) % height
        mid = [f[rows, :] for f in fields]
        y_low = [
            jnp.where(row == 0, f[before : before + 1, :], pltpu.roll(m, 1, 0))
            for f, m in zip(fields, mid)
        ]
        y_high = [
            jnp.where(row == chunk - 1, f[after : after + 1, :], pltpu.roll(m, chunk - 1, 0))
            for f, m in zip(fields, mid)
        ]
        signs = (1.0, 1.0, 1.0, -1.0, 1.0)
        z_low = [jnp.where(lane == 0, s * m, pltpu.roll(m, 1, 1)) for s, m in zip(signs, mid)]
        z_high = [jnp.where(lane == lanes - 1, m, pltpu.roll(m, lanes - 1, 1)) for m in mid]
        x_low = [low_ref[i, rows, :].astype(jnp.float32) for i in range(5)]
        x_high = [high_ref[i, rows, :].astype(jnp.float32) for i in range(5)]
        result = advance(mid, (x_low, x_high), (y_low, y_high), (z_low, z_high))
        for i in range(5):
            out_ref[i, 0, rows, :] = result[i]


def thirds(value):
    high = value.astype(jnp.bfloat16)
    rest = value - high.astype(jnp.float32)
    middle = rest.astype(jnp.bfloat16)
    low = (rest - middle.astype(jnp.float32)).astype(jnp.bfloat16)
    return high, middle, low


def couple_kernel(
    peers,
    width,
    dens_hbm,
    vel_hbm,
    press_hbm,
    owner_hbm,
    target_hbm,
    res_hbm,
    disp_hbm,
    index_hbm,
    normals_hbm,
    rbf_hbm,
    stiff_hbm,
    coup_hbm,
    inv_hbm,
    dif_hbm,
    fluid_ref,
    next_ref,
    motion_ref,
    dens_ref,
    vel_ref,
    press_ref,
    owner_ref,
    target_ref,
    res_ref,
    disp_ref,
    index_ref,
    normals_ref,
    rbf_ref,
    stiff_ref,
    coup_ref,
    inv_ref,
    dif_ref,
    ends,
    prim,
    low_ref,
    high_ref,
    side_ref,
    prior_ref,
    note_out,
    note_in,
    load_out,
    load_in,
    reply_out,
    reply_in,
    stat_out,
    stat_in,
    pick,
    place3,
    lanes_in,
    lanes_out,
    slots,
    held,
    solid,
    lines,
    fetch_sem,
    near_send,
    near_recv,
    note_sem,
    load_sem,
    stat_sem,
    reply_sem,
):
    f32, bf16 = jnp.float32, jnp.bfloat16
    me = lax.axis_index("group") * width + lax.axis_index("dev")
    blocks, nodes = index_ref.shape
    count = disp_ref.shape[1]
    columns = res_ref.shape[0]
    capacity = load_out.shape[1]
    slot_count = peers * capacity
    height, depth = dens_ref.shape[1:]
    tail = prior_ref.shape[1]
    spans = [slice(c * nodes, (c + 1) * nodes) for c in range(3)]
    half = peers // 2
    steps = sorted(range(1, peers), key=lambda d: abs(d - half))

    def hop(distance):
        return lax.rem(me + distance, peers)

    fetches = {}

    def fetch(name, src, dst):
        copy = pltpu.make_async_copy(src, dst, fetch_sem.at[len(fetches)])
        copy.start()
        fetches[name] = copy

    fetch("dens", dens_hbm, dens_ref)
    fetch("vel", vel_hbm, vel_ref)
    fetch("press", press_hbm, press_ref)
    barrier = pltpu.get_barrier_semaphore()
    for step in steps:
        pl.semaphore_signal(barrier, inc=1, device_id=hop(step), device_id_type=LOGICAL)
    fetch("owner", owner_hbm, owner_ref)
    fetch("target", target_hbm, target_ref)
    fetch("disp", disp_hbm, disp_ref)
    fetch("res", res_hbm, res_ref)
    fetch("index", index_hbm, index_ref)
    fetch("normals", normals_hbm, normals_ref)
    fetch("stiff", stiff_hbm, stiff_ref)
    fetch("coup", coup_hbm, coup_ref)
    fetch("rbf", rbf_hbm, rbf_ref)
    fetch("inv", inv_hbm, inv_ref)
    fetch("dif", dif_hbm, dif_ref)

    lanes_in[...] = jnp.zeros_like(lanes_in)
    held[...] = jnp.zeros_like(held)
    ends[...] = jnp.ones_like(ends)

    fetches["dens"].wait()
    fetches["vel"].wait()
    fetches["press"].wait()
    fields = [dens_ref.at[0]] + [vel_ref.at[i, 0] for i in range(3)] + [press_ref.at[0]]
    for i, field in enumerate(fields):
        for start in range(0, height, depth):
            part = field[start : min(start + depth, height), :]
            if part.shape[0] < depth:
                part = jnp.concatenate(
                    [part, jnp.ones((depth - part.shape[0], depth), f32)], axis=0
                )
            turned = part.T
            for z in range(2):
                ends[z, i : i + 1, start : start + depth] = turned[z : z + 1, :]
    for i, field in enumerate(fields):
        prim[i] = field[...].astype(bf16)

    edge = ends[0]
    total = edge.shape[1]
    lane = lax.broadcasted_iota(jnp.int32, edge.shape, 1)
    ahead = jnp.where(lane == height - 1, edge[:, 0:1], pltpu.roll(edge, total - 1, 1))
    behind = jnp.where(lane == 0, edge[:, height - 1 : height], pltpu.roll(edge, 1, 1))
    ends[2] = ahead
    ends[3] = behind

    def variant(ref, i):
        return [ref[i, k : k + 1, :] for k in range(5)]

    mid = variant(ends, 0)
    mirror = list(mid)
    mirror[3] = -mirror[3]
    div_y = face_difference(variant(ends, 3), mid, variant(ends, 2), 1)
    div_z = face_difference(mirror, mid, variant(ends, 1), 2)
    for i in range(5):
        ends[2, i : i + 1, :] = div_y[i] + div_z[i]

    fetches["owner"].wait()
    fetches["target"].wait()
    owner_row = owner_ref[...].astype(f32)
    target_row = target_ref[...].astype(f32)
    row_id = lax.broadcasted_iota(jnp.int32, (blocks, blocks), 0)
    column_id = lax.broadcasted_iota(jnp.int32, (blocks, blocks), 1)
    diagonal = row_id == column_id
    owner = jnp.sum(jnp.where(diagonal, owner_row, 0.0), axis=1, keepdims=True)
    target = jnp.sum(jnp.where(diagonal, target_row, 0.0), axis=1, keepdims=True)
    same = jnp.where(owner == owner_row, 1.0, 0.0)
    rank = jnp.sum(jnp.where(column_id < row_id, same, 0.0), axis=1, keepdims=True)
    rank_row = jnp.sum(jnp.where(row_id < column_id, same, 0.0), axis=0, keepdims=True)
    lane_id = lax.broadcasted_iota(jnp.int32, (blocks, slot_count), 1).astype(f32)
    pick[...] = jnp.where(owner * capacity + rank == lane_id, 1.0, 0.0).astype(bf16)
    line_id = lax.broadcasted_iota(jnp.int32, (slot_count, blocks), 0).astype(f32)
    placed = jnp.where(owner_row * capacity + rank_row == line_id, 1.0, 0.0).astype(bf16)
    for part in range(3):
        place3[:, part * blocks : (part + 1) * blocks] = placed
    mine = (me * capacity).astype(f32)
    marks = jnp.where(mine + rank == lane_id, target + 1.0, 0.0).astype(bf16)
    peer_id = lax.broadcasted_iota(jnp.int32, (peers, blocks), 0).astype(f32)
    owned = jnp.where(peer_id == owner_row, 1.0, 0.0).astype(bf16)
    tags = jnp.dot(owned, marks, preferred_element_type=f32)
    for p in range(peers):
        note_out[p, :, 0:slot_count] = tags[p : p + 1, :]

    fetches["disp"].wait()
    pl.semaphore_wait(barrier, peers - 1)

    def near(slot, src, dst, distance):
        return pltpu.make_async_remote_copy(
            src_ref=src,
            dst_ref=dst,
            send_sem=near_send.at[slot],
            recv_sem=near_recv.at[slot],
            device_id=hop(distance),
            device_id_type=LOGICAL,
        )

    wall_up = near(0, ends.at[0], side_ref.at[0], 1)
    wall_down = near(1, ends.at[0], side_ref.at[1], peers - 1)
    prior = near(2, disp_ref.at[:, pl.ds(count - tail, tail), :], prior_ref, 1)
    early, late = pl.ds(0, 3), pl.ds(3, 2)
    bulk_early = (
        near(3, prim.at[early], low_ref.at[early], 1),
        near(4, prim.at[early], high_ref.at[early], peers - 1),
    )
    bulk_late = (
        near(5, prim.at[late], low_ref.at[late], 1),
        near(6, prim.at[late], high_ref.at[late], peers - 1),
    )

    def spread(src, dst, sem, indexed):
        for step in steps:
            peer = hop(step)
            pltpu.make_async_remote_copy(
                src_ref=src.at[peer] if indexed else src,
                dst_ref=dst.at[me],
                send_sem=sem.at[0],
                recv_sem=sem.at[1],
                device_id=peer,
                device_id_type=LOGICAL,
            ).start()

    def gather(dst, sem):
        whole = dst.at[pl.ds(0, peers - 1)]
        return pltpu.make_async_remote_copy(
            src_ref=whole,
            dst_ref=whole,
            send_sem=sem.at[0],
            recv_sem=sem.at[1],
            device_id=hop(1),
            device_id_type=LOGICAL,
        )

    wall_up.start()
    wall_down.start()
    prior.start()

    fetches["res"].wait()
    for m in range(columns):
        for n in range(m, columns):
            line = jnp.sum(jnp.sum(res_ref[m] * res_ref[n], axis=0), axis=0, keepdims=True)
            lines[m * columns + n : m * columns + n + 1, :] = line
            lines[n * columns + m : n * columns + m + 1, :] = line

    def turn(value):
        kept = jnp.sum(value, axis=1, keepdims=True)
        shape = (value.shape[0], nodes)
        at = lax.broadcasted_iota(jnp.int32, shape, 0) == lax.broadcasted_iota(jnp.int32, shape, 1)
        return jnp.sum(jnp.where(at, kept, 0.0), axis=0, keepdims=True)

    gram_row = turn(lines[...])
    for p in range(peers):
        note_out[p, :, slot_count : slot_count + nodes] = gram_row
    spread(note_out, note_in, note_sem, True)
    for copy in bulk_early:
        copy.start()
    note_in[me] = note_out[me]

    for c in range(3):
        held[pl.ds(8 + c, count, stride=8), :] = disp_ref[c]
    fetches["stiff"].wait()
    fetches["coup"].wait()

    def residual(t):
        both = jnp.concatenate([held[8 * t + 8 : 8 * t + 16, :], held[8 * t : 8 * t + 8, :]], axis=1)
        weights = jnp.concatenate([stiff_ref[t], coup_ref[t]], axis=1)
        solid[8 * t : 8 * t + 8, :] = lax.dot_general(
            both.astype(bf16), weights, LAST, preferred_element_type=f32
        )

    for t in range(1, count):
        residual(t)

    fetches["index"].wait()
    fetches["normals"].wait()
    fetches["rbf"].wait()
    wall_up.wait()
    wall_down.wait()

    div_x = face_difference(variant(side_ref, 0), mid, variant(side_ref, 1), 0)
    bottom = [
        row - step_ratio * (a + ends[2, i : i + 1, :])
        for i, (row, a) in enumerate(zip(conserve(mid), div_x))
    ]
    kinetic = bottom[1] * bottom[1] + bottom[2] * bottom[2] + bottom[3] * bottom[3]
    wall = (ratio_heat - 1.0) * (bottom[4] - 0.5 * kinetic / bottom[0])

    index = index_ref[...]
    low = index % nodes
    found = jnp.zeros(index.shape, f32)
    for part in range(wall.shape[1] // nodes):
        source = jnp.broadcast_to(wall[:, part * nodes : (part + 1) * nodes], index.shape)
        taken = jnp.take_along_axis(source, low, axis=1)
        found = jnp.where(index // nodes == part, taken, found)
    for c in range(3):
        lanes_in[pl.ds(c, blocks, stride=WIDE), :] = found * normals_ref[c]

    def pair(b):
        at = WIDE * b
        return jnp.concatenate(
            [lanes_in[at : at + 8, :], lanes_in[at + 8 : at + 16, :]], axis=1
        ).astype(bf16)

    for b in range(0, blocks, 2):
        weights = rbf_ref[b : b + 2].reshape(2 * nodes, nodes)
        lanes_out[4 * b : 4 * b + 8, :] = jnp.dot(pair(b), weights, preferred_element_type=f32)
    parts = [thirds(lanes_out[pl.ds(c, blocks, stride=4), :]) for c in range(3)]
    for c in range(3):
        stack = jnp.concatenate(parts[c], axis=0)
        placed = jnp.dot(place3[...], stack, preferred_element_type=f32)
        for p in range(peers):
            load_out[p, :, spans[c]] = placed[p * capacity : (p + 1) * capacity, :]
    spread(load_out, load_in, load_sem, True)
    load_in[me] = load_out[me]

    prior.wait()
    first = (me > 0).astype(f32)
    for c in range(3):
        held[c : c + 1, :] = prior_ref[c, tail - 1 : tail, :] * first
    residual(0)

    notes = gather(note_in, note_sem)
    notes.wait_recv()
    note = jnp.sum(note_in[...], axis=0)
    tag_row = note[:, 0:slot_count]
    marked = lax.broadcasted_iota(jnp.int32, (nodes, slot_count), 0).astype(f32) + 1.0 == tag_row
    marked = jnp.where(marked, 1.0, 0.0)
    collector = marked[0:count, :].astype(bf16)
    chooser = marked.T[:, 0:count].astype(bf16)
    shape = (columns, nodes)
    m_id = lax.broadcasted_iota(jnp.int32, shape, 0)
    n_id = lax.broadcasted_iota(jnp.int32, shape, 1)
    spot = jnp.minimum(m_id * columns + n_id, nodes - 1)
    gram = jnp.broadcast_to(note[:, slot_count : slot_count + nodes], shape)
    matrix = jnp.where(
        n_id < columns,
        jnp.take_along_axis(gram, spot, axis=1),
        jnp.where(n_id == m_id + columns, 1.0, 0.0),
    )
    for k in range(columns):
        line = matrix[k : k + 1, :]
        scaled = line / matrix[k : k + 1, k : k + 1]
        matrix = jnp.where(m_id == k, scaled, matrix - matrix[:, k : k + 1] * scaled)
    fetches["inv"].wait()
    fetches["dif"].wait()

    loads = gather(load_in, load_sem)
    loads.wait_recv()
    for p in range(peers):
        slots[p * capacity : (p + 1) * capacity, :] = load_in[p]
    high, middle, rest = thirds(slots[...])
    twice = jnp.concatenate([collector, collector], axis=1)
    served = jnp.dot(
        twice, jnp.concatenate([high, middle], axis=0), preferred_element_type=f32
    ) + jnp.dot(collector, rest, preferred_element_type=f32)
    change = [
        -inv_ref[c] * (solid[pl.ds(c, count, stride=8), :] - served[:, spans[c]])
        for c in range(3)
    ]
    for m in range(columns):
        line = sum(res_ref[m, c] * change[c] for c in range(3))
        lines[m : m + 1, :] = jnp.sum(line, axis=0, keepdims=True)
    share = sum(
        -matrix[:, columns + m : columns + m + 1] * lines[m : m + 1, :] for m in range(columns)
    )
    stat_out[...] = turn(share)
    spread(stat_out, stat_in, stat_sem, False)
    for copy in bulk_late:
        copy.start()
    stat_in[me] = stat_out[...]
    base = [disp_ref[c] + change[c] for c in range(3)]
    stats = gather(stat_in, stat_sem)
    stats.wait_recv()
    mixing = jnp.broadcast_to(jnp.sum(stat_in[...], axis=0), (8, nodes))
    weights = [
        jnp.tile(jnp.broadcast_to(mixing[:, m : m + 1], (8, nodes)), (count // 8, 1))
        for m in range(columns)
    ]
    halves = []
    for c in range(3):
        result = base[c]
        for m in range(columns):
            result = result + dif_ref[m, c] * weights[m]
        next_ref[c] = result
        halves.append(result.astype(bf16))
    chosen = jnp.dot(chooser, jnp.concatenate(halves, axis=1), preferred_element_type=f32)
    for p in range(peers):
        reply_out[p] = chosen[p * capacity : (p + 1) * capacity, :].astype(bf16)
    spread(reply_out, reply_in, reply_sem, True)
    reply_in[me] = reply_out[me]

    for copy in bulk_early + bulk_late:
        copy.wait()
    flow_section(fields, low_ref, high_ref, fluid_ref)

    replies = gather(reply_in, reply_sem)
    replies.wait_recv()
    for p in range(peers):
        slots[p * capacity : (p + 1) * capacity, :] = reply_in[p].astype(f32)
    rows = jnp.dot(pick[...], slots[...].astype(bf16), preferred_element_type=f32)
    for c in range(3):
        lanes_in[pl.ds(c, blocks, stride=WIDE), :] = rows[:, spans[c]]
    for b in range(0, blocks, 2):
        weights = jnp.concatenate([rbf_ref[b], rbf_ref[b + 1]], axis=1)
        lanes_out[4 * b : 4 * b + 8, :] = lax.dot_general(
            pair(b), weights, LAST, preferred_element_type=f32
        )
    for c in range(3):
        motion_ref[c] = lanes_out[pl.ds(c, blocks, stride=4), :]
    for copy in (notes, loads, stats, replies):
        copy.wait_send()


def finish_kernel(fluid_in, next_in, motion_in, fluid_ref, next_ref, motion_ref, sems):
    pairs = ((fluid_in, fluid_ref), (next_in, next_ref), (motion_in, motion_ref))
    copies = [pltpu.make_async_copy(a, b, sems.at[i]) for i, (a, b) in enumerate(pairs)]
    for copy in copies:
        copy.start()
    for copy in copies:
        copy.wait()


def rows_last(value):
    return jnp.swapaxes(value, -3, -2)


def on_device(
    density,
    velocity,
    pressure,
    rbf_blocks,
    correlation,
    normals,
    routes,
    targets,
    stiffness,
    coupling,
    inverse_diag,
    displacement,
    diff_res,
    diff_disp,
):
    f32, bf16, i32 = jnp.float32, jnp.bfloat16, jnp.int32
    width = lax.axis_size("dev")
    peers = lax.axis_size(AXES)
    blocks, nodes = correlation.shape
    count = displacement.shape[0]
    columns = diff_res.shape[0]
    height, depth = density.shape[1:]
    capacity = max(2, 2 * blocks // peers)
    slot_count = peers * capacity
    row = 3 * nodes

    padded = -(-height // depth) * depth
    halo = (5, height, depth)
    vmem = pl.BlockSpec(memory_space=pltpu.VMEM)
    hbm = pl.BlockSpec(memory_space=pltpu.HBM)
    anywhere = pl.BlockSpec(memory_space=pl.ANY)
    dma = pltpu.SemaphoreType.DMA
    shapes = (
        jax.ShapeDtypeStruct((5,) + density.shape, f32),
        jax.ShapeDtypeStruct((3, count, nodes), f32),
        jax.ShapeDtypeStruct((3, blocks, nodes), f32),
    )
    operands = (
        density,
        velocity,
        pressure,
        routes.reshape(1, blocks),
        targets.reshape(1, blocks),
        rows_last(diff_res),
        rows_last(displacement),
        correlation,
        rows_last(normals),
        rbf_blocks,
        stiffness,
        coupling,
        rows_last(inverse_diag),
        rows_last(diff_disp),
    )
    operands = [pltpu.with_memory_space_constraint(x, pltpu.HBM) for x in operands]
    outputs = pl.pallas_call(
        functools.partial(couple_kernel, peers, width),
        out_shape=shapes,
        in_specs=[hbm] * len(operands),
        out_specs=(vmem, vmem, vmem),
        scratch_shapes=[pltpu.VMEM(x.shape, x.dtype) for x in operands]
        + [
            pltpu.VMEM((4, 8, padded), f32),
            pltpu.VMEM(halo, bf16),
            pltpu.VMEM(halo, bf16),
            pltpu.VMEM(halo, bf16),
            pltpu.VMEM((2, 8, padded), f32),
            pltpu.VMEM((3, 8, nodes), f32),
            pltpu.VMEM((peers, 1, slot_count + nodes), f32),
            pltpu.VMEM((peers, 1, slot_count + nodes), f32),
            pltpu.VMEM((peers, capacity, row), f32),
            pltpu.VMEM((peers, capacity, row), f32),
            pltpu.VMEM((peers, capacity, row), bf16),
            pltpu.VMEM((peers, capacity, row), bf16),
            pltpu.VMEM((1, nodes), f32),
            pltpu.VMEM((peers, 1, nodes), f32),
            pltpu.VMEM((blocks, slot_count), bf16),
            pltpu.VMEM((slot_count, 3 * blocks), bf16),
            pltpu.VMEM((blocks * WIDE, nodes), f32),
            pltpu.VMEM((blocks * 4, nodes), f32),
            pltpu.VMEM((slot_count, row), f32),
            pltpu.VMEM((count * 8 + 8, nodes), f32),
            pltpu.VMEM((count * 8, nodes), f32),
            pltpu.VMEM((columns * columns, nodes), f32),
            dma((len(operands),)),
            dma((7,)),
            dma((7,)),
            dma((2,)),
            dma((2,)),
            dma((2,)),
            dma((2,)),
        ],
        compiler_params=pltpu.CompilerParams(
            collective_id=0, has_side_effects=True, vmem_limit_bytes=24 * 2**20
        ),
    )(*operands)
    fluid_next, disp_next, wall_motion = pl.pallas_call(
        finish_kernel,
        out_shape=shapes,
        in_specs=[vmem] * 3,
        out_specs=(anywhere,) * 3,
        scratch_shapes=[dma((3,))],
        compiler_params=pltpu.CompilerParams(vmem_limit_bytes=16 * 2**20),
    )(*outputs)
    return (fluid_next, rows_last(disp_next), rows_last(wall_motion))


def solution(mesh):
    placed = (
        P(("group", "dev"), None, None),
        P(None, ("group", "dev"), None, None),
        P(("group", "dev"), None, None),
        P(("group", "dev"), None, None),
        P(("group", "dev"), None),
        P(("group", "dev"), None, None),
        P(("group", "dev"), None),
        P(("group", "dev")),
        P(("group", "dev"), None, None),
        P(("group", "dev"), None, None),
        P(("group", "dev"), None, None),
        P(("group", "dev"), None, None),
        P(None, ("group", "dev"), None, None),
        P(None, ("group", "dev"), None, None),
    )
    return jax.shard_map(
        on_device,
        mesh=mesh,
        in_specs=placed,
        out_specs=(
            P(None, ("group", "dev"), None, None),
            P(("group", "dev"), None, None),
            P(("group", "dev"), None, None),
        ),
        check_vma=False,
    )
```

time: 47.1 us -> 32.9 us (0.70)
  Pallas kernels: 41.2 us -> 32.1 us
  local copies, waits for them, and re-layouts: 5.05 us -> 0 us
    pallas_call x1, Pallas kernels: 38.9 us -> 31.2 us  [on_device(): pl.pallas_call(functools.partial(couple_kernel, peers, width), out_shape=...]
    unnamed x3 -> x0, local copies, waits for them, and re-layouts: 5.05 us -> none
    pallas_call x1, Pallas kernels: 2.24 us -> 0.96 us  [on_device(): pl.pallas_call(finish_kernel, out_shape=shapes, in_specs=[vmem] * 3, out_...]
where the time goes in v1:
time: 32.9 us; the launch traced here: 32.8 us
  Pallas kernels  32.1 us (98%)
  between operations  0.64 us (2%)
    pallas_call x1, Pallas kernels, on_device(): pl.pallas_call(functools.partial(couple_kernel, peers, width), out_shape=...  31.2 us
    pallas_call x1, Pallas kernels, on_device(): pl.pallas_call(finish_kernel, out_shape=shapes, in_specs=[vmem] * 3, out_...  0.96 us

profile of v1, /device:TPU:0, one launch (start us, length us, event | category | flops | bytes accessed | tf_op | source)
XLA Modules:
  0.0 32.8 jit_solution(4769921784953786729)
XLA Ops:
  0.6 31.2 %shard_map.157 = (f32[5,1,320,128]{3,2,1,0:T(8,128)S(1)}, f32[3,32,128]{2,1,0:T(8,128)S(1)}, f32[3,64,128]{2,1,0:T(8,128)S(1)}) custom-call(f32[1,320,128]{2,1,0:T(8,128)} %dens_hbm.1, f32[3,1,320,128]{3,2,1,0:T(8,128)} %vel_hbm.1, f32[1,320,128]{2,1,0:T(8,128)} %press_hbm.1, s32[1,64]{1,0:T(1,128)} %bitcast.14, s32[1,64]{1,0:T(1,128)} %bitcast.15, ...), custom_call_target="tpu_custom_call" | custom-call | tf_op jit(solution)/shard_map/pallas_call | solution.py:561
  31.8 1.0 %shard_map.158 = (f32[5,1,320,128]{3,2,1,0:T(8,128)}, f32[3,32,128]{2,1,0:T(8,128)}, f32[3,64,128]{2,1,0:T(8,128)}) custom-call(f32[5,1,320,128]{3,2,1,0:T(8,128)S(1)} %get-tuple-element.9.fluid_in, f32[3,32,128]{2,1,0:T(8,128)S(1)} %get-tuple-element.10.next_in, f32[3,64,128]{2,1,0:T(8,128)S(1)} %get-tuple-element.11.motion_in), custom_call_target="tpu_custom_call" | custom-call | tf_op jit(solution)/shard_map/pallas_call | solution.py:602

commit v2 on v1

--- a/solution.py
+++ b/solution.py
@@ -165,7 +165,8 @@
     tail = prior_ref.shape[1]
     spans = [slice(c * nodes, (c + 1) * nodes) for c in range(3)]
     half = peers // 2
-    steps = sorted(range(1, peers), key=lambda d: abs(d - half))
+    steps = sorted(range(1, peers), key=lambda d: ((d % width) // 2 != width // 4, -(d % width), d))
+    greeted = sorted(range(1, peers), key=lambda d: -abs(d - half))
 
     def hop(distance):
         return lax.rem(me + distance, peers)
@@ -181,7 +182,7 @@
     fetch("vel", vel_hbm, vel_ref)
     fetch("press", press_hbm, press_ref)
     barrier = pltpu.get_barrier_semaphore()
-    for step in steps:
+    for step in greeted:
         pl.semaphore_signal(barrier, inc=1, device_id=hop(step), device_id_type=LOGICAL)
     fetch("owner", owner_hbm, owner_ref)
     fetch("target", target_hbm, target_ref)
@@ -277,15 +278,19 @@
     wall_up = near(0, ends.at[0], side_ref.at[0], 1)
     wall_down = near(1, ends.at[0], side_ref.at[1], peers - 1)
     prior = near(2, disp_ref.at[:, pl.ds(count - tail, tail), :], prior_ref, 1)
-    early, late = pl.ds(0, 3), pl.ds(3, 2)
-    bulk_early = (
-        near(3, prim.at[early], low_ref.at[early], 1),
-        near(4, prim.at[early], high_ref.at[early], peers - 1),
-    )
-    bulk_late = (
-        near(5, prim.at[late], low_ref.at[late], 1),
-        near(6, prim.at[late], high_ref.at[late], peers - 1),
-    )
+    bulks = []
+    first_field = 0
+    for slot, amount in enumerate((1, 2, 2)):
+        part = pl.ds(first_field, amount)
+        first_field += amount
+        bulks.append(
+            (
+                near(3 + 2 * slot, prim.at[part], low_ref.at[part], 1),
+                near(4 + 2 * slot, prim.at[part], high_ref.at[part], peers - 1),
+            )
+            if amount
+            else ()
+        )
 
     def spread(src, dst, sem, indexed):
         for step in steps:
@@ -331,7 +336,7 @@
     for p in range(peers):
         note_out[p, :, slot_count : slot_count + nodes] = gram_row
     spread(note_out, note_in, note_sem, True)
-    for copy in bulk_early:
+    for copy in bulks[0]:
         copy.start()
     note_in[me] = note_out[me]
 
@@ -390,6 +395,8 @@
         for p in range(peers):
             load_out[p, :, spans[c]] = placed[p * capacity : (p + 1) * capacity, :]
     spread(load_out, load_in, load_sem, True)
+    for copy in bulks[1]:
+        copy.start()
     load_in[me] = load_out[me]
 
     prior.wait()
@@ -444,7 +451,7 @@
     )
     stat_out[...] = turn(share)
     spread(stat_out, stat_in, stat_sem, False)
-    for copy in bulk_late:
+    for copy in bulks[2]:
         copy.start()
     stat_in[me] = stat_out[...]
     base = [disp_ref[c] + change[c] for c in range(3)]
@@ -468,7 +475,7 @@
     spread(reply_out, reply_in, reply_sem, True)
     reply_in[me] = reply_out[me]
 
-    for copy in bulk_early + bulk_late:
+    for copy in bulks[0] + bulks[1] + bulks[2]:
         copy.wait()
     flow_section(fields, low_ref, high_ref, fluid_ref)
 
@@ -588,8 +595,8 @@
             pltpu.VMEM((count * 8, nodes), f32),
             pltpu.VMEM((columns * columns, nodes), f32),
             dma((len(operands),)),
-            dma((7,)),
-            dma((7,)),
+            dma((9,)),
+            dma((9,)),
             dma((2,)),
             dma((2,)),
             dma((2,)),

time: 32.9 us -> 30.8 us (0.936)
  Pallas kernels: 32.1 us -> 30 us
    pallas_call x1, Pallas kernels: 31.2 us -> 29 us  [on_device(): pl.pallas_call(functools.partial(couple_kernel, peers, width), out_shape=...]
where the time goes in v2:
time: 30.8 us; the launch traced here: 30.6 us
  Pallas kernels  30 us (97%)
  between operations  0.64 us (2%)
    pallas_call x1, Pallas kernels, on_device(): pl.pallas_call(functools.partial(couple_kernel, peers, width), out_shape=...  29 us
    pallas_call x1, Pallas kernels, on_device(): pl.pallas_call(finish_kernel, out_shape=shapes, in_specs=[vmem] * 3, out_...  0.96 us

profile of v2, /device:TPU:0, one launch (start us, length us, event | category | flops | bytes accessed | tf_op | source)
XLA Modules:
  0.0 30.6 jit_solution(13443524194816087981)
XLA Ops:
  0.6 29.0 %shard_map.157 = (f32[5,1,320,128]{3,2,1,0:T(8,128)S(1)}, f32[3,32,128]{2,1,0:T(8,128)S(1)}, f32[3,64,128]{2,1,0:T(8,128)S(1)}) custom-call(f32[1,320,128]{2,1,0:T(8,128)} %dens_hbm.1, f32[3,1,320,128]{3,2,1,0:T(8,128)} %vel_hbm.1, f32[1,320,128]{2,1,0:T(8,128)} %press_hbm.1, s32[1,64]{1,0:T(1,128)} %bitcast.14, s32[1,64]{1,0:T(1,128)} %bitcast.15, ...), custom_call_target="tpu_custom_call" | custom-call | tf_op jit(solution)/shard_map/pallas_call | solution.py:568
  29.6 1.0 %shard_map.158 = (f32[5,1,320,128]{3,2,1,0:T(8,128)}, f32[3,32,128]{2,1,0:T(8,128)}, f32[3,64,128]{2,1,0:T(8,128)}) custom-call(f32[5,1,320,128]{3,2,1,0:T(8,128)S(1)} %get-tuple-element.9.fluid_in, f32[3,32,128]{2,1,0:T(8,128)S(1)} %get-tuple-element.10.next_in, f32[3,64,128]{2,1,0:T(8,128)S(1)} %get-tuple-element.11.motion_in), custom_call_target="tpu_custom_call" | custom-call | tf_op jit(solution)/shard_map/pallas_call | solution.py:609
